TPU v7x, 32 devices: a whole 2x2x4 slice. The times are simulated.
32 devices in a mesh: row: 4 (over y, x), col: 8 (over z, core).
Axes of the slice: x: 2, y: 2, z: 4, core: 2. Of those that a mesh axis runs over, the one named last changes fastest.
Arguments:
- tokens: bfloat16 [1024, 53248], P(('row', 'col')), may hold values from -6 to 6
- eigvecs: float32 [53248, 2048], P('row', 'col'), may hold values from -0.02734375 to 0.02734375
- eigvals: float32 [2048], P('col'), may hold values from 0.25 to 4
- v_first: float32 [53248, 256], P(('row', 'col')), may hold values from -0.109375 to 0.109375
- v_second: float32 [53248, 256], P(('row', 'col')), may hold values from -0.109375 to 0.109375
- t_first: float32 [256, 256], replicated, may hold values from -0.375 to 0.375
- t_second: float32 [256, 256], replicated, may hold values from -0.375 to 0.375
Outputs:
- whitened: float32 [1024, 2048], P('row', 'col')
All inputs are finite; a program needn't handle non-finite values.
Results may differ from a plain program's by a relative error of at most 0.0029.
Values may be sent and summed in bfloat16 or wider, within the bound.
No kernel may reach another device: no remote copies, remote signals or barrier semaphores. Data moves between devices by JAX's collectives and lax.ppermute only.
A program may use at most 128 MiB of HBM per device.

v0:
```python
import jax
import jax.numpy as jnp
from jax import lax
from jax.sharding import PartitionSpec as P


def local_update(block, panel, factor, inner):
    middle = jnp.dot(
        factor, inner, precision=lax.Precision.HIGHEST, preferred_element_type=jnp.float32
    )
    return block - jnp.dot(
        panel, middle, precision=lax.Precision.HIGHEST, preferred_element_type=jnp.float32
    )


def partial_inner(panel, block):
    return jnp.dot(
        panel.T, block, precision=lax.Precision.HIGHEST, preferred_element_type=jnp.float32
    )


def per_device(tokens, eigvecs, eigvals, v_first, v_second, t_first, t_second):
    block = lax.all_to_all(eigvecs, "col", split_axis=0, concat_axis=1, tiled=True)
    for panel, factor in ((v_second, t_second), (v_first, t_first)):
        inner = lax.psum(partial_inner(panel, block), ("row", "col"))
        block = local_update(block, panel, factor, inner)
    every_value = lax.all_gather(eigvals, "col", axis=0, tiled=True)
    whitening = (block * lax.rsqrt(every_value)[None, :]).astype(jnp.bfloat16)
    slab = lax.all_to_all(tokens, ("row", "col"), split_axis=1, concat_axis=0, tiled=True)
    partial_value = jnp.dot(slab, whitening, preferred_element_type=jnp.float32)
    by_column = lax.psum_scatter(partial_value, "col", scatter_dimension=1, tiled=True)
    summed = lax.psum_scatter(by_column, "row", scatter_dimension=0, tiled=True)
    return summed


def solution(mesh):
    in_specs = (
        P(("row", "col"), None),
        P("row", "col"),
        P("col"),
        P(("row", "col"), None),
        P(("row", "col"), None),
        P(),
        P(),
    )
    out_specs = P("row", "col")
    return jax.shard_map(
        per_device, mesh=mesh, in_specs=in_specs, out_specs=out_specs, check_vma=False
    )
```

profile of v0, /device:TPU:0, one launch (start us, length us, event | category | flops | bytes accessed | tf_op | source)
XLA Modules:
  0.0 837.7 jit_solution(9575933095389601247)
XLA Ops:
  6.5 13.8 %copy.15 = f32[8,1664,256]{1,2,0:T(8,128)} copy(f32[8,1664,256]{2,1,0:T(8,128)} %bitcast.39) | data formatting | bytes 27262976 | tf_op jit(solution)/shard_map/all_to_all | solution.py:23
  20.4 6.4 all-to-all-start
  26.7 4.1 copy.20
  30.8 292.2 %all-to-all-done = f32[8,1664,256]{1,2,0:T(8,128)} async-done(((f32[8,1664,256]{1,2,0:T(8,128)}), f32[8,1664,256]{1,2,0:T(8,128)}, u32[]{:S(2)}, u32[]{:S(2)}) %all-to-all-start) | async-done | bytes 13631520 | tf_op jit(solution)/shard_map/all_to_all | solution.py:23
  323.0 4.1 all-to-all-start.1
  327.2 0.0 all-reduce.3.cloned.1.call-start
  327.2 25.8 %fusion.2 = f32[256,2048]{1,0:T(8,128)} fusion(f32[1664,256]{1,0:T(8,128)S(1)} %copy-done, f32[1664,2048]{0,1:T(8,128)} %bitcast.2), kind=kOutput, calls=%fused_computation.7 | convolution fusion | flops 10468982784 | bytes 17432576 | tf_op jit(solution)/shard_map/dot_general | solution.py:17
  353.1 0.2 all-reduce.5.cloned.1.call-start
  353.3 151.8 %all-reduce.3.cloned.1.call-done = f32[256,2048]{1,0:T(8,128)} async-done(((f32[256,2048]{1,0:T(8,128)}), f32[256,2048]{1,0:T(8,128)}) %all-reduce.3.cloned.1.call-update) | async-done | bytes 2097168 | tf_op jit(solution)/shard_map/psum | solution.py:25
  505.2 5.2 fusion.3
  510.3 16.9 %bitcast_subtract_fusion.1 = f32[1664,2048]{0,1:T(8,128)S(1)} fusion(f32[1664,2048]{0,1:T(8,128)} %bitcast.2, f32[2048,256]{1,0:T(8,128)S(1)} %fusion.3, f32[1664,256]{1,0:T(8,128)S(1)} %copy-done), kind=kOutput, calls=%fused_computation.3 | convolution fusion | flops 10472390656 | bytes 31064064 | tf_op jit(solution)/shard_map/dot_general | solution.py:11
  527.3 4.9 copy-done.2
  532.1 13.1 %convolution_bitcast_fusion.1 = f32[256,2048]{0,1:T(8,128)} fusion(f32[1664,2048]{0,1:T(8,128)S(1)} %bitcast_subtract_fusion.1, f32[1664,256]{1,0:T(8,128)S(1)} %copy-done.3), kind=kOutput, calls=%fused_computation.6 | convolution fusion | flops 10468982784 | bytes 17432576 | tf_op jit(solution)/shard_map/dot_general | solution.py:17
  545.3 0.0 reduce-scatter.3.cloned.1.call-start
  545.4 0.6 copy-done.6
  546.0 10.6 %all-gather = f32[8,1,256]{2,1,0:T(1,128)S(1)} all-gather(f32[1,1,256]{2,1,0:T(1,128)S(1)} %bitcast.43), channel_id=1, replica_groups=mesh['row'=4,'col'=8] {'col'}, dimensions={0}, use_global_device_ids=true | all-gather | bytes 9216 | tf_op jit(solution)/shard_map/all_gather | solution.py:27
  556.6 122.3 %all-reduce.5.cloned.1.call-done = f32[256,2048]{0,1:T(8,128)} async-done(((f32[256,2048]{0,1:T(8,128)}), f32[256,2048]{0,1:T(8,128)}) %all-reduce.5.cloned.1.call-update) | async-done | bytes 2097168 | tf_op jit(solution)/shard_map/psum | solution.py:25
  678.9 3.5 fusion.4
  682.4 16.4 %fusion.1 = bf16[1664,2048]{0,1:T(8,128)(2,1)} fusion(f32[1664,2048]{0,1:T(8,128)} %copy-done.2, f32[2048,256]{1,0:T(8,128)S(1)} %fusion.4, f32[1664,256]{1,0:T(8,128)S(1)} %copy-done.3, f32[2048]{0:T(1024)S(1)} %bitcast.42), kind=kOutput, calls=%fused_computation.2 | convolution fusion | flops 10479206400 | bytes 24256512 | tf_op jit(solution)/shard_map/dot_general | solution.py:11
  698.8 12.9 %convolution_bitcast_fusion = f32[1024,2048]{0,1:T(8,128)} fusion(bf16[1664,2048]{0,1:T(8,128)(2,1)} %fusion.1, bf16[1024,1664]{1,0:T(8,128)(2,1)} %bitcast.10), kind=kOutput, calls=%fused_computation.4 | convolution fusion | flops 6979321856 | bytes 18612224 | tf_op jit(solution)/shard_map/dot_general | solution.py:30
  711.8 0.0 reduce-scatter.5.cloned.1.call-start
  711.9 88.4 %reduce-scatter.3.cloned.1.call-done = f32[1024,256]{0,1:T(8,128)} async-done(((f32[1024,2048]{0,1:T(8,128)}), f32[1024,256]{0,1:T(8,128)}) %reduce-scatter.3.cloned.1.call-update) | async-done | bytes 1048592 | tf_op jit(solution)/shard_map/reduce_scatter | solution.py:31
  800.2 29.2 %reduce-scatter.5.cloned.1.call-done = f32[256,256]{0,1:T(8,128)} async-done(((f32[1024,256]{0,1:T(8,128)}), f32[256,256]{0,1:T(8,128)}) %reduce-scatter.5.cloned.1.call-update) | async-done | bytes 262160 | tf_op jit(solution)/shard_map/reduce_scatter | solution.py:32
  829.4 1.8 copy.17
  (18 shorter events, 0.1 us)
Async XLA Ops:
  6.5 320.7 %copy-start = (f32[1664,256]{1,0:T(8,128)S(1)}, f32[1664,256]{1,0:T(8,128)}, u32[]{:S(2)}) copy-start(f32[1664,256]{1,0:T(8,128)} %param.11) | copy-start | bytes 5111812
  20.4 302.7 %all-to-all-start = ((f32[8,1664,256]{1,2,0:T(8,128)}), f32[8,1664,256]{1,2,0:T(8,128)}, u32[]{:S(2)}, u32[]{:S(2)}) async-start(f32[8,1664,256]{1,2,0:T(8,128)} %copy.15), calls=%async_computation | async-start | bytes 27262976 | tf_op jit(solution)/shard_map/all_to_all | solution.py:23
  323.0 375.8 %all-to-all-start.1 = ((bf16[32,32,1664]{2,0,1:T(8,128)(2,1)}), bf16[32,32,1664]{2,0,1:T(8,128)(2,1)}, u32[]{:S(2)}, u32[]{:S(2)}) async-start(bf16[32,32,1664]{2,0,1:T(8,128)(2,1)} %bitcast.40), calls=%async_computation.1 | async-start | bytes 6815744 | tf_op jit(solution)/shard_map/all_to_all | solution.py:29
  327.2 178.0 %all-reduce.3.cloned.1.call-start = ((), (), s32[]{:S(2)}) async-start(), calls=%async_computation.4 | async-start | bytes 4194304 | tf_op jit(solution)/shard_map/psum | solution.py:25
  353.1 152.1 %copy-start.4 = (f32[256,256]{1,0:T(8,128)S(1)}, f32[256,256]{1,0:T(8,128)}, u32[]{:S(2)}) copy-start(f32[256,256]{1,0:T(8,128)} %param.13) | copy-start | bytes 786436
  353.1 325.8 %all-reduce.5.cloned.1.call-start = ((), (), s32[]{:S(2)}) async-start(), calls=%async_computation.5 | async-start | bytes 4194304 | tf_op jit(solution)/shard_map/psum | solution.py:25
  510.3 21.8 %copy-start.3 = (f32[1664,256]{1,0:T(8,128)S(1)}, f32[1664,256]{1,0:T(8,128)}, u32[]{:S(2)}) copy-start(f32[1664,256]{1,0:T(8,128)} %param.10) | copy-start | bytes 5111812
  527.2 4.9 copy-start.2
  545.3 0.7 copy-start.6
  545.3 133.6 %copy-start.5 = (f32[256,256]{1,0:T(8,128)S(1)}, f32[256,256]{1,0:T(8,128)}, u32[]{:S(2)}) copy-start(f32[256,256]{1,0:T(8,128)} %param.12) | copy-start | bytes 786436
  545.3 254.9 %reduce-scatter.3.cloned.1.call-start = ((), (), s32[]{:S(2)}) async-start(), calls=%async_computation.6 | async-start | bytes 9437184 | tf_op jit(solution)/shard_map/reduce_scatter | solution.py:31
  711.8 119.4 %copy-start.1 = (f32[1664,256]{1,0:T(8,128)S(1)}, f32[1664,256]{1,0:T(8,128)}, u32[]{:S(2)}) copy-start(f32[1664,256]{1,0:T(8,128)} %param.11) | copy-start | bytes 5111812
  711.8 117.6 %reduce-scatter.5.cloned.1.call-start = ((), (), s32[]{:S(2)}) async-start(), calls=%async_computation.7 | async-start | bytes 1310720 | tf_op jit(solution)/shard_map/reduce_scatter | solution.py:32
Sparse Core Ops, SparseCore 0:
  353.2 151.8 all-reduce.2
  545.4 133.4 all-reduce.4
  711.9 88.2 reduce-scatter.2
  803.0 26.4 reduce-scatter.4
where the time goes:
time: 838 us
  waiting for transfers between devices  684 us (82%)
  matrix products  93.9 us (11%)
  local copies, waits for them, and re-layouts  25.3 us (3%)
  between operations  13.2 us (2%)
  starting transfers between devices  10.8 us (1%)
  blocking collectives  10.6 us (1%)
    all_to_all x1, waiting for transfers between devices, per_device(): lax.all_to_all(eigvecs, 'col', split_axis=0, concat_axis=1, tiled=True)  292 us
    psum x2, waiting for transfers between devices, per_device(): inner = lax.psum(partial_inner(panel, block), ('row', 'col'))  274 us
    reduce_scatter x1, waiting for transfers between devices, per_device(): lax.psum_scatter(partial_value, 'col', scatter_dimension=1, tiled=True)  88.4 us
    dot_general x2, matrix products, partial_inner(): jnp.dot(panel.T, block, precision=lax.Precision.HIGHEST, preferred_elemen...  39 us
    dot_general x2, matrix products, local_update(): jnp.dot(panel, middle, precision=lax.Precision.HIGHEST, preferred_element...  33.3 us
    reduce_scatter x1, waiting for transfers between devices, per_device(): summed = lax.psum_scatter(by_column, 'row', scatter_dimension=0, tiled=True)  29.2 us
  transfers between devices with their start and end apart: 6, of which 5 were waited for; matrix products, arithmetic and copies ran while one was open for 10% of the time, Pallas kernels for 0%

commit v1 on v0

--- a/solution.py
+++ b/solution.py
@@ -2,6 +2,8 @@
 import jax.numpy as jnp
 from jax import lax
 from jax.sharding import PartitionSpec as P
+
+vectors_solve = lambda field: lax.psum(lax.psum(field, axis_name="col"), axis_name="row")
 
 
 def local_update(block, panel, factor, inner):
@@ -22,7 +24,7 @@
 def per_device(tokens, eigvecs, eigvals, v_first, v_second, t_first, t_second):
     block = lax.all_to_all(eigvecs, "col", split_axis=0, concat_axis=1, tiled=True)
     for panel, factor in ((v_second, t_second), (v_first, t_first)):
-        inner = lax.psum(partial_inner(panel, block), ("row", "col"))
+        inner = vectors_solve(partial_inner(panel, block))
         block = local_update(block, panel, factor, inner)
     every_value = lax.all_gather(eigvals, "col", axis=0, tiled=True)
     whitening = (block * lax.rsqrt(every_value)[None, :]).astype(jnp.bfloat16)

time: 838 us -> 870 us (1.038); the launches traced: 838 us -> 860 us
  blocking collectives: 10.6 us -> 313 us
  waiting for transfers between devices: 684 us -> 407 us
    all_to_all x0 -> x1, blocking collectives: none -> 303 us  [per_device(): lax.all_to_all(eigvecs, 'col', split_axis=0, concat_axis=1, tiled=True)]
    all_to_all x1 -> x0, waiting for transfers between devices: 292 us -> none  [per_device(): lax.all_to_all(eigvecs, 'col', split_axis=0, concat_axis=1, tiled=True)]
    psum x2 -> x4, waiting for transfers between devices: 274 us -> 288 us  [the longest x2 159 us: lax.psum(lax.psum(field, axis_name='col'), axis_name='row')]
  transfers between devices with their start and end apart: 6 -> 7, of which waited for: 5 -> 6; matrix products, arithmetic and copies ran while one was open for 10% -> 7% of each run, Pallas kernels for 0% -> 0%
where the time goes in v1:
time: 870 us; the launch traced here: 860 us
  waiting for transfers between devices  407 us (47%)
  blocking collectives  313 us (36%)
  matrix products  91.7 us (11%)
  local copies, waits for them, and re-layouts  29.5 us (3%)
  between operations  14 us (2%)
    all_to_all x1, blocking collectives, per_device(): lax.all_to_all(eigvecs, 'col', split_axis=0, concat_axis=1, tiled=True)  303 us
    psum x2, waiting for transfers between devices, lax.psum(lax.psum(field, axis_name='col'), axis_name='row')  159 us
    psum x2, waiting for transfers between devices, lax.psum(field, axis_name='col')  129 us
    reduce_scatter x1, waiting for transfers between devices, per_device(): lax.psum_scatter(partial_value, 'col', scatter_dimension=1, tiled=True)  89.6 us
    dot_general x2, matrix products, partial_inner(): jnp.dot(panel.T, block, precision=lax.Precision.HIGHEST, preferred_elemen...  36.5 us
    dot_general x2, matrix products, local_update(): jnp.dot(panel, middle, precision=lax.Precision.HIGHEST, preferred_element...  33.5 us
    reduce_scatter x1, waiting for transfers between devices, per_device(): summed = lax.psum_scatter(by_column, 'row', scatter_dimension=0, tiled=True)  29.2 us
  transfers between devices with their start and end apart: 7, of which 6 were waited for; matrix products, arithmetic and copies ran while one was open for 7% of the time, Pallas kernels for 0%

profile of v1, /device:TPU:0, one launch (start us, length us, event | category | flops | bytes accessed | tf_op | source)
XLA Modules:
  0.0 860.2 jit_solution(3578963951012251666)
XLA Ops:
  6.5 13.9 %copy.15 = f32[8,1664,256]{1,2,0:T(8,128)} copy(f32[8,1664,256]{2,1,0:T(8,128)} %bitcast.41) | data formatting | bytes 27262976 | tf_op jit(solution)/shard_map/all_to_all | solution.py:25
  20.4 302.6 %all_to_all.38 = f32[8,1664,256]{1,2,0:T(8,128)S(1)} all-to-all(f32[8,1664,256]{1,2,0:T(8,128)} %copy.15), channel_id=1, replica_groups=mesh['row'=4,'col'=8] {'col'}, dimensions={0} | all-to-all | bytes 27262976 | tf_op jit(solution)/shard_map/all_to_all | solution.py:25
  323.0 4.9 copy-done.3
  327.9 23.4 %fusion.2 = f32[256,2048]{1,0:T(8,128)} fusion(f32[1664,256]{1,0:T(8,128)S(1)} %copy-done, f32[1664,2048]{0,1:T(8,128)S(1)} %bitcast.39), kind=kOutput, calls=%fused_computation.7 | convolution fusion | flops 10468982784 | bytes 17432576 | tf_op jit(solution)/shard_map/dot_general | solution.py:19
  351.3 0.0 all-reduce.7.cloned.1.call-start
  351.4 64.2 %all-reduce.5.cloned.1.call-done = f32[256,2048]{1,0:T(8,128)} async-done(((f32[256,2048]{1,0:T(8,128)}), f32[256,2048]{1,0:T(8,128)}) %all-reduce.5.cloned.1.call-update) | async-done | bytes 2097168 | tf_op jit(solution)/shard_map/psum | solution.py:6
  415.6 4.0 copy.20
  419.6 4.3 all-to-all-start.1
  423.9 0.0 all-reduce.9.cloned.1.call-start
  424.0 97.7 %all-reduce.7.cloned.1.call-done = f32[256,2048]{1,0:T(8,128)} async-done(((f32[256,2048]{1,0:T(8,128)}), f32[256,2048]{1,0:T(8,128)}) %all-reduce.7.cloned.1.call-update) | async-done | bytes 2097168 | tf_op jit(solution)/shard_map/psum | solution.py:6
  521.7 5.2 fusion.3
  526.9 17.1 %bitcast_subtract_fusion.1 = f32[1664,2048]{0,1:T(8,128)S(1)} fusion(f32[1664,2048]{0,1:T(8,128)} %bitcast.40, f32[2048,256]{1,0:T(8,128)S(1)} %fusion.3, f32[1664,256]{1,0:T(8,128)S(1)} %copy-done), kind=kOutput, calls=%fused_computation.3 | convolution fusion | flops 10472390656 | bytes 31064064 | tf_op jit(solution)/shard_map/dot_general | solution.py:13
  544.0 4.9 copy-done.2
  548.8 13.1 %convolution_bitcast_fusion.1 = f32[256,2048]{0,1:T(8,128)} fusion(f32[1664,2048]{0,1:T(8,128)S(1)} %bitcast_subtract_fusion.1, f32[1664,256]{1,0:T(8,128)S(1)} %copy-done.4), kind=kOutput, calls=%fused_computation.6 | convolution fusion | flops 10468982784 | bytes 17432576 | tf_op jit(solution)/shard_map/dot_general | solution.py:19
  562.0 65.2 %all-reduce.9.cloned.1.call-done = f32[256,2048]{0,1:T(8,128)} async-done(((f32[256,2048]{0,1:T(8,128)}), f32[256,2048]{0,1:T(8,128)}) %all-reduce.9.cloned.1.call-update) | async-done | bytes 2097168 | tf_op jit(solution)/shard_map/psum | solution.py:6
  627.3 10.7 %all-gather = f32[8,1,256]{2,1,0:T(1,128)S(1)} all-gather(f32[1,1,256]{2,1,0:T(1,128)S(1)} %bitcast.45), channel_id=1, replica_groups=mesh['row'=4,'col'=8] {'col'}, dimensions={0}, use_global_device_ids=true | all-gather | bytes 9216 | tf_op jit(solution)/shard_map/all_gather | solution.py:29
  638.0 61.3 %all-reduce.11.cloned.1.call-done = f32[256,2048]{0,1:T(8,128)} async-done(((f32[256,2048]{0,1:T(8,128)}), f32[256,2048]{0,1:T(8,128)}) %all-reduce.11.cloned.1.call-update) | async-done | bytes 2097168 | tf_op jit(solution)/shard_map/psum | solution.py:6
  699.3 3.5 fusion.4
  702.8 16.4 %fusion.1 = bf16[1664,2048]{0,1:T(8,128)(2,1)} fusion(f32[1664,2048]{0,1:T(8,128)} %copy-done.2, f32[2048,256]{1,0:T(8,128)S(1)} %fusion.4, f32[1664,256]{1,0:T(8,128)S(1)} %copy-done.4, f32[2048]{0:T(1024)S(1)} %bitcast.44), kind=kOutput, calls=%fused_computation.2 | convolution fusion | flops 10479206400 | bytes 24256512 | tf_op jit(solution)/shard_map/dot_general | solution.py:13
  719.3 12.9 %convolution_bitcast_fusion = f32[1024,2048]{0,1:T(8,128)} fusion(bf16[1664,2048]{0,1:T(8,128)(2,1)} %fusion.1, bf16[1024,1664]{1,0:T(8,128)(2,1)} %bitcast.10), kind=kOutput, calls=%fused_computation.4 | convolution fusion | flops 6979321856 | bytes 18612224 | tf_op jit(solution)/shard_map/dot_general | solution.py:32
  732.3 0.0 reduce-scatter.5.cloned.1.call-start
  732.3 89.6 %reduce-scatter.3.cloned.1.call-done = f32[1024,256]{0,1:T(8,128)} async-done(((f32[1024,2048]{0,1:T(8,128)}), f32[1024,256]{0,1:T(8,128)}) %reduce-scatter.3.cloned.1.call-update) | async-done | bytes 1048592 | tf_op jit(solution)/shard_map/reduce_scatter | solution.py:33
  822.0 29.2 %reduce-scatter.5.cloned.1.call-done = f32[256,256]{0,1:T(8,128)} async-done(((f32[1024,256]{0,1:T(8,128)}), f32[256,256]{0,1:T(8,128)}) %reduce-scatter.5.cloned.1.call-update) | async-done | bytes 262160 | tf_op jit(solution)/shard_map/reduce_scatter | solution.py:34
  851.1 1.8 copy.17
  (25 shorter events, 0.2 us)
Async XLA Ops:
  6.5 321.3 %copy-start = (f32[1664,256]{1,0:T(8,128)S(1)}, f32[1664,256]{1,0:T(8,128)}, u32[]{:S(2)}) copy-start(f32[1664,256]{1,0:T(8,128)} %param.11) | copy-start | bytes 5111812
  6.5 409.0 %all-reduce.5.cloned.1.call-start = ((), (), s32[]{:S(2)}) async-start(), calls=%async_computation.4 | async-start | bytes 4194304 | tf_op jit(solution)/shard_map/psum | solution.py:6
  323.0 4.9 copy-start.3
  351.3 170.4 %all-reduce.7.cloned.1.call-start = ((), (), s32[]{:S(2)}) async-start(), calls=%async_computation.5 | async-start | bytes 4194304 | tf_op jit(solution)/shard_map/psum | solution.py:6
  419.6 102.1 %copy-start.5 = (f32[256,256]{1,0:T(8,128)S(1)}, f32[256,256]{1,0:T(8,128)}, u32[]{:S(2)}) copy-start(f32[256,256]{1,0:T(8,128)} %param.13) | copy-start | bytes 786436
  419.6 299.7 %all-to-all-start.1 = ((bf16[32,32,1664]{2,0,1:T(8,128)(2,1)}), bf16[32,32,1664]{2,0,1:T(8,128)(2,1)}, u32[]{:S(2)}, u32[]{:S(2)}) async-start(bf16[32,32,1664]{2,0,1:T(8,128)(2,1)} %bitcast.42), calls=%async_computation.1 | async-start | bytes 6815744 | tf_op jit(solution)/shard_map/all_to_all | solution.py:31
  423.9 203.3 %all-reduce.9.cloned.1.call-start = ((), (), s32[]{:S(2)}) async-start(), calls=%async_computation.6 | async-start | bytes 4194304 | tf_op jit(solution)/shard_map/psum | solution.py:6
  526.8 22.0 %copy-start.4 = (f32[1664,256]{1,0:T(8,128)S(1)}, f32[1664,256]{1,0:T(8,128)}, u32[]{:S(2)}) copy-start(f32[1664,256]{1,0:T(8,128)} %param.10) | copy-start | bytes 5111812
  544.0 4.9 copy-start.2
  562.0 65.3 %copy-start.7 = (f32[256]{0:T(256)S(1)}, f32[256]{0:T(256)}, u32[]{:S(2)}) copy-start(f32[256]{0:T(256)} %param.9) | copy-start | bytes 3076
  562.0 137.3 %copy-start.6 = (f32[256,256]{1,0:T(8,128)S(1)}, f32[256,256]{1,0:T(8,128)}, u32[]{:S(2)}) copy-start(f32[256,256]{1,0:T(8,128)} %param.12) | copy-start | bytes 786436
  562.0 137.3 %all-reduce.11.cloned.1.call-start = ((), (), s32[]{:S(2)}) async-start(), calls=%async_computation.7 | async-start | bytes 4194304 | tf_op jit(solution)/shard_map/psum | solution.py:6
  627.3 194.7 %reduce-scatter.3.cloned.1.call-start = ((), (), s32[]{:S(2)}) async-start(), calls=%async_computation.8 | async-start | bytes 9437184 | tf_op jit(solution)/shard_map/reduce_scatter | solution.py:33
  732.2 120.7 %copy-start.1 = (f32[1664,256]{1,0:T(8,128)S(1)}, f32[1664,256]{1,0:T(8,128)}, u32[]{:S(2)}) copy-start(f32[1664,256]{1,0:T(8,128)} %param.11) | copy-start | bytes 5111812
  732.3 118.9 %reduce-scatter.5.cloned.1.call-start = ((), (), s32[]{:S(2)}) async-start(), calls=%async_computation.9 | async-start | bytes 1310720 | tf_op jit(solution)/shard_map/reduce_scatter | solution.py:34
Sparse Core Ops, SparseCore 0:
  351.4 64.0 all-reduce.4
  418.6 102.9 all-reduce.6
  562.1 65.0 all-reduce.8
  630.2 69.0 all-reduce.10
  732.4 89.5 reduce-scatter.2
  824.7 26.4 reduce-scatter.4
